TPU v7x, 256 devices: a whole 4x4x8 slice. The times are simulated.
256 devices in a mesh: seq: 32 (over z, y), exp: 8 (over x, core).
Axes of the slice: x: 4, y: 4, z: 8, core: 2. Of those that a mesh axis runs over, the one named last changes fastest.
Arguments:
- resid_rows: bfloat16 [8, 128, 3072], P('exp', 'seq'), may hold values from -6 to 6
- query_rows: bfloat16 [8, 128, 3072], P('exp', 'seq'), may hold values from -6 to 6
- key_rows: bfloat16 [8, 4096, 3072], P('exp', 'seq'), may hold values from -6 to 6
- value_rows: bfloat16 [8, 4096, 3072], P('exp', 'seq'), may hold values from -6 to 6
- log_decay: float32 [8, 48, 4096], P('exp', None, 'seq'), may hold values from -1 to 0
- read_pos: int32 [8, 128], P('exp', 'seq'), may hold values from 0 to 4095, as said below
- expert_ids: int32 [8, 128, 2], P('exp', 'seq'), may hold values from 0 to 7, all different within a row; in each aligned block of 4 rows (0 to 3, 4 to 7, ..., all dimensions but the last counted through in order) at most 2 rows name the same one
- pair_order: int32 [8], replicated, may hold values from 0 to 7, each once
- lengths: int32 [8], replicated, may hold values from 1 to 4096
- norm_gain: bfloat16 [3072], replicated, may hold values from 0.5 to 1.5
- router_weight: bfloat16 [3072, 8], replicated, may hold values from -0.109375 to 0.109375
- score_weight: bfloat16 [3072], replicated, may hold values from -0.109375 to 0.109375
- gate_weight: bfloat16 [8, 3072, 9216], P('exp', None, 'seq'), may hold values from -0.109375 to 0.109375
- up_weight: bfloat16 [8, 3072, 9216], P('exp', None, 'seq'), may hold values from -0.109375 to 0.109375
- down_weight: bfloat16 [8, 9216, 3072], P('exp', 'seq'), may hold values from -0.0625 to 0.0625
Outputs:
- pair_loss: float32 [], replicated
- grad_query: float32 [8, 128, 3072], P('exp', 'seq')
- grad_resid: float32 [8, 128, 3072], P('exp', 'seq')
- grad_keys: bfloat16 [8, 4096, 3072], P('exp', 'seq')
- grad_values: bfloat16 [8, 4096, 3072], P('exp', 'seq')
Inputs may be any that keep to these rules, and one draw needn't show every extreme that they name: `read_pos`: each aligned block j of 4 entries of a sequence holds strictly increasing positions from j * 128 to (j + 1) * 128 - 1, the last of them being (j + 1) * 128 - 1. `expert_ids`: the two entries of a row differ; in the rows of one device (aligned blocks of 4 rows) no expert is named by more than 2 rows. `pair_order`: each sequence appears once.
All inputs are finite; a program needn't handle non-finite values.
Results may differ from a plain program's by a relative error of at most 0.018.
Values may be sent and summed in bfloat16 or wider, within the bound.
No kernel may reach another device: no remote copies, remote signals or barrier semaphores. Data moves between devices by JAX's collectives and lax.ppermute only.
A program may use at most 128 MiB of HBM per device.

v0:
```python
import jax
import jax.numpy as jnp
from jax import lax
from jax.sharding import PartitionSpec as P

PRECISE = lax.Precision.HIGHEST
EPSILON = 1e-06
LENGTH_WEIGHT = 4.0
SCORE_SCALE = 256.0


def carried_in(value, axis, join, neutral, backward):
    count = lax.axis_size(axis)
    place = lax.axis_index(axis)
    ahead = count - 1 - place if backward else place
    gathered = jax.tree.map(
        lambda a, kind: lax.all_gather(a.astype(kind), axis), value, (jnp.bfloat16, jnp.bfloat16)
    )
    state = jax.tree.map(lambda a, e: jnp.zeros_like(a) + jnp.asarray(e, a.dtype), value, neutral)

    def one(lap, state):
        source = count - 1 - lap if backward else lap
        return join(
            state,
            jax.tree.map(
                lambda a, own: lax.dynamic_index_in_dim(a, source, 0, False).astype(own.dtype),
                gathered,
                value,
            ),
        )

    return lax.fori_loop(0, ahead, one, state)


def merge_states(earlier, later):
    return (earlier[0] * later[0], later[0][:, None, None] * earlier[1] + later[1])


def chain_prefix(decay, summary, backwards):
    blank = (jnp.ones_like(decay), jnp.zeros_like(summary))
    joined = carried_in((decay, summary), "seq", merge_states, blank, backwards)
    return joined[1]


def readout_weights(cumulated, places):
    positions = jnp.arange(cumulated.shape[1], dtype=jnp.int32)
    one_hot = (places[:, None] == positions[None, :]).astype(jnp.float32)
    at_read = jnp.dot(cumulated, one_hot.T, precision=PRECISE)
    allowed = positions[None, :] <= places[:, None]
    exponent = jnp.where(allowed[None], at_read[:, :, None] - cumulated[:, None, :], -1e30)
    return (at_read, jnp.exp(exponent))


def preference_loss(rewards, pair_order, lengths, total_length):
    count = rewards.shape[0]
    ordering = (pair_order[:, None] == jnp.arange(count, dtype=jnp.int32)[None, :]).astype(
        jnp.float32
    )
    ranked = jnp.dot(ordering, rewards, precision=PRECISE).reshape(count // 2, 2)
    fitted = jnp.mean(jax.nn.softplus(ranked[:, 1] - ranked[:, 0]))
    share = lengths.astype(jnp.float32) / total_length
    scatter_breadth = jnp.mean((rewards - jnp.mean(rewards)) * (share - jnp.mean(share)))
    return fitted + LENGTH_WEIGHT * scatter_breadth * scatter_breadth


def to_experts(slots):
    return lax.all_to_all(slots, "exp", split_axis=0, concat_axis=0, tiled=True)


def over_slots(arrived, project):
    return project(lax.all_gather(arrived, "seq", axis=0, tiled=True), jnp.int32(0))


def collect(project, expert_count, capacity):
    slot_count = expert_count * capacity
    summed = lax.psum_scatter(
        project(jnp.int32(0), slot_count * lax.axis_size("seq")).astype(jnp.bfloat16),
        "seq",
        scatter_dimension=0,
        tiled=True,
    )
    shaped = summed.reshape(expert_count, capacity, -1)
    return lax.all_to_all(shaped, "exp", split_axis=0, concat_axis=0, tiled=True)


def per_device(
    resid_rows,
    query_rows,
    key_rows,
    value_rows,
    log_decay,
    read_pos,
    expert_ids,
    pair_order,
    lengths,
    norm_gain,
    router_weight,
    score_weight,
    gate_weight,
    up_weight,
    down_weight,
):
    seq_count = lax.axis_size("seq")
    exp_count = lax.axis_size("exp")
    seq_index = lax.axis_index("seq")
    exp_index = lax.axis_index("exp")
    token_count = key_rows.shape[1]
    model_width = key_rows.shape[2]
    head_count = log_decay.shape[1]
    head_size = model_width // head_count
    read_count = query_rows.shape[1]
    expert_count = router_weight.shape[1]
    capacity = max(2, 4 * read_count // exp_count)
    keys_half = key_rows[0].reshape(token_count, head_count, head_size)
    values_half = value_rows[0].reshape(token_count, head_count, head_size)
    query_half = query_rows[0].reshape(read_count, head_count, head_size)
    keys_float = keys_half.astype(jnp.float32)
    values_float = values_half.astype(jnp.float32)
    query_float = query_half.astype(jnp.float32)
    cumulated = jnp.cumsum(log_decay[0], axis=1)
    group_decay = jnp.exp(cumulated[:, -1])
    tail_decay = jnp.exp(cumulated[:, -1:] - cumulated).T[:, :, None]
    own_state = jnp.einsum("thi,thj->hij", keys_float * tail_decay, values_float, precision=PRECISE)
    state_in = chain_prefix(group_decay, own_state, False)
    places = read_pos[0] - seq_index * token_count
    at_read, weight = readout_weights(cumulated, places)
    lift = jnp.exp(at_read).T[:, :, None]
    query_key = (
        jnp.einsum("rhi,thi->hrt", query_half, keys_half, preferred_element_type=jnp.float32)
        / head_size
    )
    attended = jnp.einsum("hrt,thj->rhj", weight * query_key, values_float, precision=PRECISE)
    attended = (
        attended
        + lift * jnp.einsum("rhi,hij->rhj", query_float, state_in, precision=PRECISE) / head_size
    )
    residual = resid_rows[0].astype(jnp.float32) + attended.reshape(read_count, model_width)
    inverse = lax.rsqrt(jnp.mean(residual * residual, axis=1, keepdims=True) + EPSILON)
    unit_rows = residual * inverse
    gain_float = norm_gain.astype(jnp.float32)
    normed = (unit_rows * gain_float).astype(jnp.bfloat16)
    logits = jnp.dot(normed, router_weight, preferred_element_type=jnp.float32)
    picks = (
        expert_ids[0][:, :, None] == jnp.arange(expert_count, dtype=jnp.int32)[None, None, :]
    ).astype(jnp.float32)
    chosen = jnp.einsum("rke,re->rk", picks, logits, precision=PRECISE)
    first = jax.nn.sigmoid(chosen[:, 0] - chosen[:, 1])
    gates = jnp.stack([first, 1.0 - first], axis=1)
    flat = picks.reshape(read_count * 2, expert_count)
    earlier = jnp.cumsum(flat, axis=0) - flat
    slot_index = jnp.sum(earlier * flat, axis=1)
    slot_hot = (slot_index[:, None] == jnp.arange(capacity, dtype=jnp.float32)[None, :]).astype(
        jnp.float32
    )
    placement = (
        (flat[:, :, None] * slot_hot[:, None, :])
        .reshape(read_count * 2, expert_count * capacity)
        .astype(jnp.bfloat16)
    )
    doubled = jnp.repeat(normed, 2, axis=0)
    outgoing = jnp.dot(placement.T, doubled, preferred_element_type=jnp.float32).astype(
        jnp.bfloat16
    )
    arrived = to_experts(outgoing.reshape(expert_count, capacity, model_width)).reshape(
        expert_count * capacity, model_width
    )
    gate_w = gate_weight[0]
    up_w = up_weight[0]
    down_w = down_weight[0]
    hidden_count = gate_w.shape[1]

    def project_in(piece, start):
        gate_part = jnp.dot(piece, gate_w, preferred_element_type=jnp.float32)
        up_part = jnp.dot(piece, up_w, preferred_element_type=jnp.float32)
        return jnp.concatenate([gate_part, up_part], axis=1)

    projected = over_slots(arrived, project_in)
    pre_gate = projected[:, :hidden_count]
    pre_up = projected[:, hidden_count:]
    gate_sigmoid = jax.nn.sigmoid(pre_gate)
    activated = (pre_gate * gate_sigmoid * pre_up).astype(jnp.bfloat16)

    def project_out(start, count):
        return jnp.dot(activated, down_w, preferred_element_type=jnp.float32)

    returned = collect(project_out, expert_count, capacity)
    expert_out = jnp.dot(
        placement,
        returned.reshape(expert_count * capacity, model_width),
        preferred_element_type=jnp.float32,
    )
    expert_out = expert_out.reshape(read_count, 2, model_width)
    mixed = residual + jnp.sum(gates[:, :, None] * expert_out, axis=1)
    score_float = score_weight.astype(jnp.float32)
    score = jnp.dot(mixed, score_float, precision=PRECISE)
    own_total = jnp.sum(score) / (read_count * seq_count)
    marked = jnp.where(jnp.arange(exp_count) == exp_index, own_total, 0.0)
    rewards = lax.psum(marked, ("seq", "exp"))
    pair_loss, d_reward = jax.value_and_grad(preference_loss)(
        rewards, pair_order, lengths, token_count * seq_count
    )
    own_grad = jnp.sum(jnp.where(jnp.arange(exp_count) == exp_index, d_reward, 0.0)) * SCORE_SCALE
    d_mixed = jnp.broadcast_to((own_grad * score_float)[None, :], (read_count, model_width))
    d_out = (gates[:, :, None] * d_mixed[:, None, :]).astype(jnp.bfloat16)
    d_gates = jnp.einsum("rd,rkd->rk", d_mixed, expert_out, precision=PRECISE)
    d_logit = (d_gates[:, 0] - d_gates[:, 1]) * first * (1.0 - first)
    back_out = jnp.dot(
        placement.T, d_out.reshape(read_count * 2, model_width), preferred_element_type=jnp.float32
    ).astype(jnp.bfloat16)
    back_arrived = to_experts(back_out.reshape(expert_count, capacity, model_width)).reshape(
        expert_count * capacity, model_width
    )

    def project_back(piece, start):
        return jnp.einsum("sd,fd->sf", piece, down_w, preferred_element_type=jnp.float32)

    d_act = over_slots(back_arrived, project_back)
    d_pre_gate = (d_act * pre_up * gate_sigmoid * (1.0 + pre_gate * (1.0 - gate_sigmoid))).astype(
        jnp.bfloat16
    )
    d_pre_up = (d_act * pre_gate * gate_sigmoid).astype(jnp.bfloat16)

    def project_in_back(start, count):
        gate_term = jnp.einsum("sf,df->sd", d_pre_gate, gate_w, preferred_element_type=jnp.float32)
        up_term = jnp.einsum("sf,df->sd", d_pre_up, up_w, preferred_element_type=jnp.float32)
        return gate_term + up_term

    d_in_slots = collect(project_in_back, expert_count, capacity)
    d_in = jnp.dot(
        placement,
        d_in_slots.reshape(expert_count * capacity, model_width),
        preferred_element_type=jnp.float32,
    )
    d_in = d_in.reshape(read_count, 2, model_width)
    columns = jnp.einsum("rke,de->rkd", picks, router_weight.astype(jnp.float32), precision=PRECISE)
    d_normed = jnp.sum(d_in, axis=1) + d_logit[:, None] * (columns[:, 0] - columns[:, 1])
    d_unit = d_normed * gain_float
    grad_resid = d_mixed + inverse * (
        d_unit - unit_rows * jnp.mean(d_unit * unit_rows, axis=1, keepdims=True)
    )
    rounded = grad_resid.astype(jnp.bfloat16)
    d_half = rounded.reshape(read_count, head_count, head_size)
    d_attended = d_half.astype(jnp.float32)
    summary = (
        jnp.einsum("rhi,rhj->hij", query_float * lift, d_attended, precision=PRECISE) / head_size
    )
    suffix = chain_prefix(group_decay, summary, True)
    grad_dot = (
        jnp.einsum("rhj,thj->hrt", d_half, values_half, preferred_element_type=jnp.float32)
        / head_size
    )
    grad_query = jnp.einsum("hrt,thi->rhi", weight * grad_dot, keys_float, precision=PRECISE)
    grad_query = (
        grad_query
        + lift * jnp.einsum("rhj,hij->rhi", d_attended, state_in, precision=PRECISE) / head_size
    )
    grad_keys = jnp.einsum("hrt,rhi->thi", weight * grad_dot, query_float, precision=PRECISE)
    grad_keys = grad_keys + tail_decay * jnp.einsum(
        "hij,thj->thi", suffix, values_float, precision=PRECISE
    )
    grad_values = jnp.einsum("hrt,rhj->thj", weight * query_key, d_attended, precision=PRECISE)
    grad_values = grad_values + tail_decay * jnp.einsum(
        "thi,hij->thj", keys_float, suffix, precision=PRECISE
    )
    return (
        pair_loss,
        grad_query.reshape(1, read_count, model_width),
        grad_resid.reshape(1, read_count, model_width),
        grad_keys.reshape(1, token_count, model_width).astype(jnp.bfloat16),
        grad_values.reshape(1, token_count, model_width).astype(jnp.bfloat16),
    )


def solution(mesh):
    in_specs = (
        P("exp", "seq", None),
        P("exp", "seq", None),
        P("exp", "seq", None),
        P("exp", "seq", None),
        P("exp", None, "seq"),
        P("exp", "seq"),
        P("exp", "seq", None),
        P(),
        P(),
        P(),
        P(),
        P(),
        P("exp", None, "seq"),
        P("exp", None, "seq"),
        P("exp", "seq", None),
    )
    out_specs = (
        P(),
        P("exp", "seq", None),
        P("exp", "seq", None),
        P("exp", "seq", None),
        P("exp", "seq", None),
    )
    return jax.shard_map(
        per_device, mesh=mesh, in_specs=in_specs, out_specs=out_specs, check_vma=False
    )
```

profile of v0, /device:TPU:1, one launch (start us, length us, event | category | flops | bytes accessed | tf_op | source)
XLA Modules:
  0.0 1303.2 jit_solution(8809889284805440682)
XLA Ops:
  8.7 1.5 copy.58
  10.2 1.8 copy.60
  12.1 2.2 fusion.17
  16.3 65.9 %all-reduce.2 = bf16[1536]{0:T(1024)(128)(2,1)S(1)} all-reduce(bf16[1536]{0:T(1024)(128)(2,1)S(1)} %dynamic-update-slice), channel_id=2, replica_groups=mesh['seq'=32,'exp'=8] {'seq'}, use_global_device_ids=true, to_apply=%add.2 | all-reduce | flops 1536 | bytes 6144
  87.4 2.0 convolution_bitcast_fusion.3
  89.4 111.9 %all-gather.12.cloned.1.call-done = bf16[1536,64,64]{2,1,0:T(8,128)(2,1)} async-done(((bf16[48,64,64]{2,1,0:T(8,128)(2,1)}), bf16[1536,64,64]{2,1,0:T(8,128)(2,1)}) %all-gather.12.cloned.1.call-update) | async-done | bytes 12582928 | tf_op jit(solution)/shard_map/all_gather | solution.py:17
  201.5 1.8 multiply_reduce_fusion.1
  204.4 1.6 reshape.388
  209.6 1.6 convolution_convert_fusion.2
  211.2 1.6 reshape.390
  212.8 10.7 all_to_all.20
  223.5 1.6 reshape.391
  225.1 137.3 %all-gather.8.cloned.1.call-done = bf16[512,3072]{1,0:T(8,128)(2,1)} async-done(((bf16[16,3072]{1,0:T(8,128)(2,1)}), bf16[512,3072]{1,0:T(8,128)(2,1)}) %all-gather.8.cloned.1.call-update) | async-done | bytes 3145744 | tf_op jit(solution)/shard_map/all_gather | solution.py:71
  362.4 3.7 fusion.8
  368.3 3.5 convolution_convert_fusion
  382.1 207.1 %reduce-scatter.3.cloned.1.call-done = bf16[16,3072]{1,0:T(8,128)(2,1)} async-done(((bf16[512,3072]{1,0:T(8,128)(2,1)}), bf16[16,3072]{1,0:T(8,128)(2,1)}) %reduce-scatter.3.cloned.1.call-update) | async-done | bytes 98320 | tf_op jit(solution)/shard_map/reduce_scatter | solution.py:76
  589.2 1.6 reshape.392
  590.8 10.0 all-to-all-start.1
  603.3 2.6 all-to-all-done.1
  605.9 1.6 reshape.419
  607.4 1.7 multiply_reduce_fusion
  609.1 1.7 fusion.32
  613.3 74.1 %psum.7 = f32[8]{0:T(128)} all-reduce(f32[8]{0:T(128)} %compare_select_fusion.4), channel_id=1, replica_groups=mesh['seq'=32,'exp'=8] {'seq','exp'}, use_global_device_ids=true, to_apply=%region_9.10 | all-reduce | flops 8 | bytes 64 | tf_op jit(solution)/shard_map/psum | solution.py:198
  696.0 1.5 fusion.85
  702.9 1.5 convolution_convert_fusion.1
  704.4 1.6 reshape.396
  705.9 9.6 all_to_all.21
  715.5 1.6 reshape.397
  717.2 72.2 %all-gather.10.cloned.1.call-done = bf16[512,3072]{1,0:T(8,128)(2,1)} async-done(((bf16[16,3072]{1,0:T(8,128)(2,1)}), bf16[512,3072]{1,0:T(8,128)(2,1)}) %all-gather.10.cloned.1.call-update) | async-done | bytes 3145744 | tf_op jit(solution)/shard_map/all_gather | solution.py:71
  789.4 3.1 fusion
  792.6 2.0 fusion.6
  794.7 3.7 add_convert_fusion
  800.2 215.3 %reduce-scatter.5.cloned.1.call-done = bf16[16,3072]{1,0:T(8,128)(2,1)} async-done(((bf16[512,3072]{1,0:T(8,128)(2,1)}), bf16[16,3072]{1,0:T(8,128)(2,1)}) %reduce-scatter.5.cloned.1.call-update) | async-done | bytes 98320 | tf_op jit(solution)/shard_map/reduce_scatter | solution.py:76
  1015.6 1.6 reshape.398
  1017.2 10.0 all-to-all-start.3
  1027.3 4.9 all-to-all-done.3
  1033.6 3.2 multiply_convert_fusion
  1044.5 2.0 fusion.62
  1046.5 2.0 fusion.88
  1049.3 167.0 %all-gather.14.cloned.1.call-done = bf16[1536,64,64]{2,1,0:T(8,128)(2,1)} async-done(((bf16[48,64,64]{2,1,0:T(8,128)(2,1)}), bf16[1536,64,64]{2,1,0:T(8,128)(2,1)}) %all-gather.14.cloned.1.call-update) | async-done | bytes 12582928 | tf_op jit(solution)/shard_map/all_gather | solution.py:17
  1216.5 68.8 %while.27 = (s32[]{:T(128)}, f32[48,64,64]{2,1,0:T(8,128)S(1)}, s32[]{:T(128)}, bf16[32,48]{1,0:T(8,128)(2,1)}, bf16[32,48,64,64]{3,2,1,0:T(8,128)(2,1)}, /*index=5*/s32[]{:T(128)}, s32[]{:T(128)}, s32[]{:T(128)}, s32[]{:T(128)}) while((s32[]{:T(128)}, f32[48,64,64]{2,1,0:T(8,128)S(1)}, s32[]{:T(128)}, bf16[32,48]{1,0:T(8,128)(2,1)}, ...), condition=%wide.region_20.21_spmd, body=%wide.region_19.20_spmd.sunk | while | flops 589878 | bytes 1966715 | solution.py:32
  1217.2 1.5 convert_add_fusion.5
  1219.4 1.5 convert_add_fusion.5
  1221.6 1.5 convert_add_fusion.5
  1223.8 1.5 convert_add_fusion.5
  1226.1 1.5 convert_add_fusion.5
  1228.3 1.5 convert_add_fusion.5
  1230.5 1.5 convert_add_fusion.5
  1232.7 1.5 convert_add_fusion.5
  1234.9 1.5 convert_add_fusion.5
  1237.1 1.5 convert_add_fusion.5
  1239.3 1.5 convert_add_fusion.5
  1241.5 1.5 convert_add_fusion.5
  1243.7 1.5 convert_add_fusion.5
  1245.9 1.5 convert_add_fusion.5
  1248.1 1.5 convert_add_fusion.5
  1250.3 1.5 convert_add_fusion.5
  1252.6 1.5 convert_add_fusion.5
  1254.8 1.5 convert_add_fusion.5
  1257.0 1.5 convert_add_fusion.5
  1261.4 1.5 convert_add_fusion.5
  1285.3 2.4 fusion.13
  1288.9 4.1 fusion.11
  1293.0 2.3 copy.78
  (238 shorter events, 88.9 us)
Async XLA Ops:
  7.2 361.1 %copy-start = (bf16[1,288,3072]{2,1,0:T(8,128)(2,1)S(1)}, bf16[1,288,3072]{2,1,0:T(8,128)(2,1)}, u32[]{:S(2)}) copy-start(bf16[1,288,3072]{2,1,0:T(8,128)(2,1)} %param.33) | copy-start | bytes 5308420
  7.2 194.1 %all-gather.12.cloned.1.call-start = ((), (), s32[]{:S(2)}) async-start(), calls=%async_computation.10 | async-start | bytes 25952256 | tf_op jit(solution)/shard_map/all_gather | solution.py:17
  8.4 77.3 %copy-start.24 = (f32[48,128]{1,0:T(8,128)}, f32[48,128]{1,0:T(8,128)S(1)}, u32[]{:S(2)}) copy-start(f32[48,128]{1,0:T(8,128)S(1)} %reduce_window_sum.22) | copy-start | bytes 73732
  8.7 3.3 copy-start.21
  10.2 75.5 %copy-start.2 = (bf16[1,128,3072]{1,2,0:T(8,128)(2,1)}, bf16[1,128,3072]{1,2,0:T(8,128)(2,1)S(1)}, u32[]{:S(2)}) copy-start(bf16[1,128,3072]{1,2,0:T(8,128)(2,1)S(1)} %copy.58) | copy-start | bytes 2359300
  12.0 74.8 %copy-start.4 = (bf16[1,128,3072]{1,2,0:T(8,128)(2,1)}, bf16[1,128,3072]{1,2,0:T(8,128)(2,1)S(1)}, u32[]{:S(2)}) copy-start(bf16[1,128,3072]{1,2,0:T(8,128)(2,1)S(1)} %copy.60) | copy-start | bytes 2359300
  12.0 2.4 copy-start.40
  12.0 2.6 copy-start.37
  12.0 2.6 copy-start.50
  12.0 70.9 %copy-start.49 = (s32[1,4]{1,0:T(1,128)S(1)}, s32[1,4]{1,0:T(1,128)}, u32[]{:S(2)}) copy-start(s32[1,4]{1,0:T(1,128)} %param.24) | copy-start | bytes 52
  12.1 72.5 %copy-start.36 = (bf16[1,4,3072]{2,1,0:T(4,128)(2,1)S(1)}, bf16[1,4,3072]{2,1,0:T(4,128)(2,1)}, u32[]{:S(2)}) copy-start(bf16[1,4,3072]{2,1,0:T(4,128)(2,1)} %param.20) | copy-start | bytes 73732
  12.1 72.6 %copy-start.25 = (bf16[1,4,3072]{2,1,0:T(4,128)(2,1)S(1)}, bf16[1,4,3072]{2,1,0:T(4,128)(2,1)}, u32[]{:S(2)}) copy-start(bf16[1,4,3072]{2,1,0:T(4,128)(2,1)} %param.19) | copy-start | bytes 73732
  14.3 348.1 %all-gather.8.cloned.1.call-start = ((), (), s32[]{:S(2)}) async-start(), calls=%async_computation.6 | async-start | bytes 3244032 | tf_op jit(solution)/shard_map/all_gather | solution.py:71
  82.9 0.9 copy-start.51
  84.6 116.8 %copy-start.12 = (bf16[4,48,64]{2,1,0:T(8,128)(2,1)}, bf16[4,48,64]{2,1,0:T(8,128)(2,1)S(1)}, u32[]{:S(2)}) copy-start(bf16[4,48,64]{2,1,0:T(8,128)(2,1)S(1)} %reshape_squeeze.9) | copy-start | bytes 73732
  85.7 115.8 %copy-start.52 = (pred[4,128]{1,0:T(4,128)(4,1)}, pred[4,128]{1,0:T(4,128)(4,1)S(1)}, u32[]{:S(2)}) copy-start(pred[4,128]{1,0:T(4,128)(4,1)S(1)} %iota_compare_fusion.6) | copy-start | bytes 1540
  86.8 0.6 copy-start.28
  206.9 0.6 copy-start.33
  225.1 364.1 %reduce-scatter.3.cloned.1.call-start = ((), (), s32[]{:S(2)}) async-start(), calls=%async_computation.7 | async-start | bytes 3244032 | tf_op jit(solution)/shard_map/reduce_scatter | solution.py:76
  362.4 3.7 copy-start.9
  362.4 3.9 copy-start.48
  366.3 1.1 copy-start.6
  367.4 0.8 copy-start.16
  590.8 15.1 %all-to-all-start.1 = ((bf16[8,2,3072]{2,1,0:T(2,128)(2,1)}), bf16[8,2,3072]{2,1,0:T(2,128)(2,1)}, u32[]{:S(2)}, u32[]{:S(2)}) async-start(bf16[8,2,3072]{2,1,0:T(2,128)(2,1)} %reshape.392), calls=%async_computation.2 | async-start | bytes 196608 | tf_op jit(solution)/shard_map/all_to_all | solution.py:83
  600.8 188.6 %all-gather.10.cloned.1.call-start = ((), (), s32[]{:S(2)}) async-start(), calls=%async_computation.8 | async-start | bytes 3244032 | tf_op jit(solution)/shard_map/all_gather | solution.py:71
  702.3 0.6 copy-start.30
  717.1 298.5 %reduce-scatter.5.cloned.1.call-start = ((), (), s32[]{:S(2)}) async-start(), calls=%async_computation.9 | async-start | bytes 3244032 | tf_op jit(solution)/shard_map/reduce_scatter | solution.py:76
  789.4 3.2 copy-start.7
  789.4 3.2 copy-start.8
  789.4 3.2 copy-start.17
  792.6 2.0 copy-start.10
  798.3 0.7 copy-start.38
  798.3 0.8 copy-start.35
  798.3 0.8 copy-start.41
  798.3 1.0 copy-start.31
  798.3 1.0 copy-start.34
  798.3 228.8 %copy-start.45 = (f32[4,1]{0,1:T(1,128)S(1)}, f32[4,1]{0,1:T(1,128)}, u32[]{:S(2)}) copy-start(f32[4,1]{0,1:T(1,128)} %get-tuple-element.175) | copy-start | bytes 52
  798.4 233.9 %copy-start.39 = (bf16[4,2,16]{2,0,1:T(4,128)(2,1)S(1)}, bf16[4,2,16]{2,0,1:T(4,128)(2,1)}, u32[]{:S(2)}) copy-start(bf16[4,2,16]{2,0,1:T(4,128)(2,1)} %copy.67) | copy-start | bytes 772
  798.4 234.1 %copy-start.18 = (f32[4,3072]{1,0:T(4,128)S(1)}, f32[4,3072]{1,0:T(4,128)}, u32[]{:S(2)}) copy-start(f32[4,3072]{1,0:T(4,128)} %reshape.388) | copy-start | bytes 147460
  798.4 234.1 %copy-start.26 = (bf16[1,4,3072]{2,1,0:T(4,128)(2,1)S(1)}, bf16[1,4,3072]{2,1,0:T(4,128)(2,1)}, u32[]{:S(2)}) copy-start(bf16[1,4,3072]{2,1,0:T(4,128)(2,1)} %param.19) | copy-start | bytes 73732
  798.4 234.1 %copy-start.42 = (f32[4]{0:T(128)S(1)}, f32[4]{0:T(128)}, u32[]{:S(2)}) copy-start(f32[4]{0:T(128)} %add_rsqrt_fusion) | copy-start | bytes 52
  799.0 234.5 %copy-start.13 = (bf16[4,48,64]{2,1,0:T(8,128)(2,1)S(1)}, bf16[4,48,64]{2,1,0:T(8,128)(2,1)}, u32[]{:S(2)}) copy-start(bf16[4,48,64]{2,1,0:T(8,128)(2,1)} %copy-done.12) | copy-start | bytes 73732
  1017.2 15.0 %all-to-all-start.3 = ((bf16[8,2,3072]{2,1,0:T(2,128)(2,1)}), bf16[8,2,3072]{2,1,0:T(2,128)(2,1)S(1)}, u32[]{:S(2)}, u32[]{:S(2)}) async-start(bf16[8,2,3072]{2,1,0:T(2,128)(2,1)} %reshape.398), calls=%async_computation.5 | async-start | bytes 196608 | tf_op jit(solution)/shard_map/all_to_all | solution.py:83
  1027.2 189.1 %all-gather.14.cloned.1.call-start = ((), (), s32[]{:S(2)}) async-start(), calls=%async_computation.11 | async-start | bytes 25952256 | tf_op jit(solution)/shard_map/all_gather | solution.py:17
  1027.2 5.9 copy-start.43
  1027.3 9.5 copy-start.11
  1032.2 7.7 copy-start.5
  1032.4 0.6 copy-start.14
  1032.7 0.6 copy-start.19
  1032.8 0.6 copy-start.46
  1033.5 7.5 copy-start.3
  1036.7 5.6 copy-start.23
  1042.3 4.1 copy-start.29
  1044.4 4.1 copy-start.15
  1044.4 4.1 copy-start.20
  1044.4 4.1 copy-start.27
  1044.4 4.1 copy-start.32
  1044.4 4.1 copy-start.44
  1044.5 4.1 copy-start.47
  1216.5 68.8 %copy-start.22 = (f32[128,48]{0,1:T(8,128)S(1)}, f32[128,48]{0,1:T(8,128)}, u32[]{:S(2)}) copy-start(f32[128,48]{0,1:T(8,128)} %copy-done.21) | copy-start | bytes 73732
  1288.9 6.4 copy-start.1
Sparse Core Ops, SparseCore 0:
  14.5 186.7 all-gather.11
  225.2 137.1 all-gather.7
  371.9 217.2 reduce-scatter.2
  717.3 72.1 all-gather.9
  798.5 216.9 reduce-scatter.4
  1036.9 179.3 all-gather.13
where the time goes:
time: 1310 us; the launch traced here: 1300 us
  waiting for transfers between devices  918 us (70%)
  blocking collectives  160 us (12%)
  other arithmetic  85.5 us (7%)
  matrix products  54 us (4%)
  local copies, waits for them, and re-layouts  41.1 us (3%)
  between operations  22.6 us (2%)
  starting transfers between devices  20.2 us (2%)
    reduce_scatter x2, waiting for transfers between devices, collect(): lax.psum_scatter(project(jnp.int32(0), slot_count * lax.axis_size('seq'))...  422 us
    all_gather x2, waiting for transfers between devices, carried_in(): lax.all_gather(a.astype(kind), axis)  279 us
    all_gather x2, waiting for transfers between devices, over_slots(): lax.all_gather(arrived, 'seq', axis=0, tiled=True)  210 us
    psum x1, blocking collectives, per_device(): rewards = lax.psum(marked, ('seq', 'exp'))  74.1 us
    unnamed x1, blocking collectives  65.9 us
    add x31, other arithmetic, merge_states(): later[0][:, None, None] * earlier[1] + later[1]  46.5 us
  transfers between devices with their start and end apart: 8, of which 8 were waited for; matrix products, arithmetic and copies ran while one was open for 2% of the time, Pallas kernels for 0%

commit v1 on v0

--- a/solution.py
+++ b/solution.py
@@ -195,7 +195,9 @@
     score = jnp.dot(mixed, score_float, precision=PRECISE)
     own_total = jnp.sum(score) / (read_count * seq_count)
     marked = jnp.where(jnp.arange(exp_count) == exp_index, own_total, 0.0)
-    rewards = lax.psum(marked, ("seq", "exp"))
+    rewards = marked
+    for nth in ("exp", "seq"):
+        rewards = lax.psum(rewards, nth)
     pair_loss, d_reward = jax.value_and_grad(preference_loss)(
         rewards, pair_order, lengths, token_count * seq_count
     )

time: 1310 us -> 1320 us (level)
    all_to_all x2, blocking collectives: 20.3 us -> 34.5 us  [to_experts(): return lax.all_to_all(slots, 'exp', split_axis=0, concat_axis=0, tiled=True)]
    psum x1 -> x2, blocking collectives: 74.1 us -> 72.2 us  [per_device(): rewards = lax.psum(rewards, nth)]
where the time goes in v1:
time: 1320 us
  waiting for transfers between devices  919 us (70%)
  blocking collectives  173 us (13%)
  other arithmetic  85.9 us (7%)
  matrix products  54.1 us (4%)
  local copies, waits for them, and re-layouts  41.5 us (3%)
  between operations  22.9 us (2%)
  starting transfers between devices  20.2 us (2%)
    reduce_scatter x2, waiting for transfers between devices, collect(): lax.psum_scatter(project(jnp.int32(0), slot_count * lax.axis_size('seq'))...  423 us
    all_gather x2, waiting for transfers between devices, carried_in(): lax.all_gather(a.astype(kind), axis)  279 us
    all_gather x2, waiting for transfers between devices, over_slots(): lax.all_gather(arrived, 'seq', axis=0, tiled=True)  209 us
    psum x2, blocking collectives, per_device(): rewards = lax.psum(rewards, nth)  72.2 us
    unnamed x1, blocking collectives  65.9 us
    add x31, other arithmetic, merge_states(): later[0][:, None, None] * earlier[1] + later[1]  46.5 us
    all_to_all x2, blocking collectives, to_experts(): return lax.all_to_all(slots, 'exp', split_axis=0, concat_axis=0, tiled=True)  34.5 us
  transfers between devices with their start and end apart: 8, of which 8 were waited for; matrix products, arithmetic and copies ran while one was open for 2% of the time, Pallas kernels for 0%

profile of v1, /device:TPU:1, one launch (start us, length us, event | category | flops | bytes accessed | tf_op | source)
XLA Modules:
  0.0 1317.1 jit_solution(17880184684053869841)
XLA Ops:
  8.7 1.5 copy.58
  10.2 1.8 copy.60
  12.1 2.2 fusion.17
  16.3 65.9 %all-reduce.2 = bf16[1536]{0:T(1024)(128)(2,1)S(1)} all-reduce(bf16[1536]{0:T(1024)(128)(2,1)S(1)} %dynamic-update-slice), channel_id=2, replica_groups=mesh['seq'=32,'exp'=8] {'seq'}, use_global_device_ids=true, to_apply=%add.2 | all-reduce | flops 1536 | bytes 6144
  87.4 2.0 convolution_bitcast_fusion.3
  89.4 111.9 %all-gather.12.cloned.1.call-done = bf16[1536,64,64]{2,1,0:T(8,128)(2,1)} async-done(((bf16[48,64,64]{2,1,0:T(8,128)(2,1)}), bf16[1536,64,64]{2,1,0:T(8,128)(2,1)}) %all-gather.12.cloned.1.call-update) | async-done | bytes 12582928 | tf_op jit(solution)/shard_map/all_gather | solution.py:17
  201.5 1.8 multiply_reduce_fusion.1
  204.5 1.6 reshape.388
  209.7 1.6 convolution_convert_fusion.2
  211.3 1.6 reshape.390
  212.9 10.7 all_to_all.20
  223.6 1.6 reshape.391
  225.2 137.3 %all-gather.8.cloned.1.call-done = bf16[512,3072]{1,0:T(8,128)(2,1)} async-done(((bf16[16,3072]{1,0:T(8,128)(2,1)}), bf16[512,3072]{1,0:T(8,128)(2,1)}) %all-gather.8.cloned.1.call-update) | async-done | bytes 3145744 | tf_op jit(solution)/shard_map/all_gather | solution.py:71
  362.5 3.7 fusion.8
  368.4 3.6 convolution_convert_fusion
  382.5 207.0 %reduce-scatter.3.cloned.1.call-done = bf16[16,3072]{1,0:T(8,128)(2,1)} async-done(((bf16[512,3072]{1,0:T(8,128)(2,1)}), bf16[16,3072]{1,0:T(8,128)(2,1)}) %reduce-scatter.3.cloned.1.call-update) | async-done | bytes 98320 | tf_op jit(solution)/shard_map/reduce_scatter | solution.py:76
  589.6 1.6 reshape.392
  591.1 9.7 all-to-all-start.1
  602.1 3.8 all-to-all-done.1
  605.9 1.6 reshape.419
  607.4 1.7 multiply_reduce_fusion
  609.1 1.7 fusion.32
  613.3 13.2 %psum.14 = f32[8]{0:T(128)} all-reduce(f32[8]{0:T(128)} %compare_select_fusion.4), channel_id=1, replica_groups=mesh['seq'=32,'exp'=8] {'exp'}, use_global_device_ids=true, to_apply=%region_9.10 | all-reduce | flops 8 | bytes 64 | tf_op jit(solution)/shard_map/psum | solution.py:200
  627.8 59.0 %psum.15 = f32[8]{0:T(128)} all-reduce(f32[8]{0:T(128)} %psum.14), channel_id=1, replica_groups=mesh['seq'=32,'exp'=8] {'seq'}, use_global_device_ids=true, to_apply=%region_10.11 | all-reduce | flops 8 | bytes 64 | tf_op jit(solution)/shard_map/psum | solution.py:200
  695.8 1.6 fusion.85
  699.4 1.5 fusion.31
  702.9 1.5 convolution_convert_fusion.1
  704.4 1.6 reshape.396
  706.0 23.8 %all_to_all.21 = bf16[8,2,3072]{2,1,0:T(2,128)(2,1)} all-to-all(bf16[8,2,3072]{2,1,0:T(2,128)(2,1)} %reshape.396), channel_id=1, replica_groups=mesh['seq'=32,'exp'=8] {'exp'}, dimensions={0} | all-to-all | bytes 196608 | tf_op jit(solution)/shard_map/all_to_all | solution.py:67
  729.8 1.6 reshape.397
  731.6 71.3 %all-gather.10.cloned.1.call-done = bf16[512,3072]{1,0:T(8,128)(2,1)} async-done(((bf16[16,3072]{1,0:T(8,128)(2,1)}), bf16[512,3072]{1,0:T(8,128)(2,1)}) %all-gather.10.cloned.1.call-update) | async-done | bytes 3145744 | tf_op jit(solution)/shard_map/all_gather | solution.py:71
  802.9 3.1 fusion
  806.1 2.0 fusion.6
  808.2 3.7 add_convert_fusion
  813.8 215.6 %reduce-scatter.5.cloned.1.call-done = bf16[16,3072]{1,0:T(8,128)(2,1)} async-done(((bf16[512,3072]{1,0:T(8,128)(2,1)}), bf16[16,3072]{1,0:T(8,128)(2,1)}) %reduce-scatter.5.cloned.1.call-update) | async-done | bytes 98320 | tf_op jit(solution)/shard_map/reduce_scatter | solution.py:76
  1029.4 1.6 reshape.398
  1030.9 10.2 all-to-all-start.3
  1041.2 4.9 all-to-all-done.3
  1047.5 3.2 multiply_convert_fusion
  1058.5 2.0 fusion.62
  1060.5 2.0 fusion.88
  1063.3 166.8 %all-gather.14.cloned.1.call-done = bf16[1536,64,64]{2,1,0:T(8,128)(2,1)} async-done(((bf16[48,64,64]{2,1,0:T(8,128)(2,1)}), bf16[1536,64,64]{2,1,0:T(8,128)(2,1)}) %all-gather.14.cloned.1.call-update) | async-done | bytes 12582928 | tf_op jit(solution)/shard_map/all_gather | solution.py:17
  1230.3 68.8 %while.27 = (s32[]{:T(128)}, f32[48,64,64]{2,1,0:T(8,128)S(1)}, s32[]{:T(128)}, bf16[32,48]{1,0:T(8,128)(2,1)}, bf16[32,48,64,64]{3,2,1,0:T(8,128)(2,1)}, /*index=5*/s32[]{:T(128)}, s32[]{:T(128)}, s32[]{:T(128)}, s32[]{:T(128)}) while((s32[]{:T(128)}, f32[48,64,64]{2,1,0:T(8,128)S(1)}, s32[]{:T(128)}, bf16[32,48]{1,0:T(8,128)(2,1)}, ...), condition=%wide.region_21.22_spmd, body=%wide.region_20.21_spmd.sunk | while | flops 589878 | bytes 1966715 | solution.py:32
  1231.0 1.5 convert_add_fusion.5
  1233.2 1.5 convert_add_fusion.5
  1235.4 1.5 convert_add_fusion.5
  1237.7 1.5 convert_add_fusion.5
  1239.9 1.5 convert_add_fusion.5
  1242.1 1.5 convert_add_fusion.5
  1244.3 1.5 convert_add_fusion.5
  1246.5 1.5 convert_add_fusion.5
  1248.7 1.5 convert_add_fusion.5
  1251.0 1.5 convert_add_fusion.5
  1253.2 1.5 convert_add_fusion.5
  1255.4 1.5 convert_add_fusion.5
  1257.6 1.5 convert_add_fusion.5
  1259.8 1.5 convert_add_fusion.5
  1262.0 1.5 convert_add_fusion.5
  1264.2 1.5 convert_add_fusion.5
  1266.4 1.5 convert_add_fusion.5
  1284.2 1.5 convert_add_fusion.5
  1299.1 2.4 fusion.13
  1302.7 4.1 fusion.11
  1306.8 2.3 copy.78
  (239 shorter events, 91.5 us)
Async XLA Ops:
  7.2 361.2 %copy-start = (bf16[1,288,3072]{2,1,0:T(8,128)(2,1)S(1)}, bf16[1,288,3072]{2,1,0:T(8,128)(2,1)}, u32[]{:S(2)}) copy-start(bf16[1,288,3072]{2,1,0:T(8,128)(2,1)} %param.33) | copy-start | bytes 5308420
  7.2 194.1 %all-gather.12.cloned.1.call-start = ((), (), s32[]{:S(2)}) async-start(), calls=%async_computation.10 | async-start | bytes 25952256 | tf_op jit(solution)/shard_map/all_gather | solution.py:17
  8.4 77.3 %copy-start.24 = (f32[48,128]{1,0:T(8,128)}, f32[48,128]{1,0:T(8,128)S(1)}, u32[]{:S(2)}) copy-start(f32[48,128]{1,0:T(8,128)S(1)} %reduce_window_sum.22) | copy-start | bytes 73732
  8.7 3.3 copy-start.21
  10.2 75.5 %copy-start.2 = (bf16[1,128,3072]{1,2,0:T(8,128)(2,1)}, bf16[1,128,3072]{1,2,0:T(8,128)(2,1)S(1)}, u32[]{:S(2)}) copy-start(bf16[1,128,3072]{1,2,0:T(8,128)(2,1)S(1)} %copy.58) | copy-start | bytes 2359300
  12.0 74.8 %copy-start.4 = (bf16[1,128,3072]{1,2,0:T(8,128)(2,1)}, bf16[1,128,3072]{1,2,0:T(8,128)(2,1)S(1)}, u32[]{:S(2)}) copy-start(bf16[1,128,3072]{1,2,0:T(8,128)(2,1)S(1)} %copy.60) | copy-start | bytes 2359300
  12.0 2.4 copy-start.40
  12.0 2.6 copy-start.37
  12.0 2.6 copy-start.50
  12.0 70.9 %copy-start.49 = (s32[1,4]{1,0:T(1,128)S(1)}, s32[1,4]{1,0:T(1,128)}, u32[]{:S(2)}) copy-start(s32[1,4]{1,0:T(1,128)} %param.24) | copy-start | bytes 52
  12.1 72.5 %copy-start.36 = (bf16[1,4,3072]{2,1,0:T(4,128)(2,1)S(1)}, bf16[1,4,3072]{2,1,0:T(4,128)(2,1)}, u32[]{:S(2)}) copy-start(bf16[1,4,3072]{2,1,0:T(4,128)(2,1)} %param.20) | copy-start | bytes 73732
  12.1 72.6 %copy-start.25 = (bf16[1,4,3072]{2,1,0:T(4,128)(2,1)S(1)}, bf16[1,4,3072]{2,1,0:T(4,128)(2,1)}, u32[]{:S(2)}) copy-start(bf16[1,4,3072]{2,1,0:T(4,128)(2,1)} %param.19) | copy-start | bytes 73732
  14.3 348.2 %all-gather.8.cloned.1.call-start = ((), (), s32[]{:S(2)}) async-start(), calls=%async_computation.6 | async-start | bytes 3244032 | tf_op jit(solution)/shard_map/all_gather | solution.py:71
  82.9 0.9 copy-start.51
  84.7 116.8 %copy-start.12 = (bf16[4,48,64]{2,1,0:T(8,128)(2,1)}, bf16[4,48,64]{2,1,0:T(8,128)(2,1)S(1)}, u32[]{:S(2)}) copy-start(bf16[4,48,64]{2,1,0:T(8,128)(2,1)S(1)} %reshape_squeeze.9) | copy-start | bytes 73732
  85.7 115.8 %copy-start.52 = (pred[4,128]{1,0:T(4,128)(4,1)}, pred[4,128]{1,0:T(4,128)(4,1)S(1)}, u32[]{:S(2)}) copy-start(pred[4,128]{1,0:T(4,128)(4,1)S(1)} %iota_compare_fusion.6) | copy-start | bytes 1540
  86.8 0.6 copy-start.28
  207.0 0.6 copy-start.33
  225.2 364.4 %reduce-scatter.3.cloned.1.call-start = ((), (), s32[]{:S(2)}) async-start(), calls=%async_computation.7 | async-start | bytes 3244032 | tf_op jit(solution)/shard_map/reduce_scatter | solution.py:76
  362.5 3.7 copy-start.9
  362.5 3.9 copy-start.48
  366.4 1.1 copy-start.6
  367.6 0.8 copy-start.16
  591.1 14.7 %all-to-all-start.1 = ((bf16[8,2,3072]{2,1,0:T(2,128)(2,1)}), bf16[8,2,3072]{2,1,0:T(2,128)(2,1)}, u32[]{:S(2)}, u32[]{:S(2)}) async-start(bf16[8,2,3072]{2,1,0:T(2,128)(2,1)} %reshape.392), calls=%async_computation.2 | async-start | bytes 196608 | tf_op jit(solution)/shard_map/all_to_all | solution.py:83
  600.8 202.2 %all-gather.10.cloned.1.call-start = ((), (), s32[]{:S(2)}) async-start(), calls=%async_computation.8 | async-start | bytes 3244032 | tf_op jit(solution)/shard_map/all_gather | solution.py:71
  702.3 0.6 copy-start.30
  731.4 298.0 %reduce-scatter.5.cloned.1.call-start = ((), (), s32[]{:S(2)}) async-start(), calls=%async_computation.9 | async-start | bytes 3244032 | tf_op jit(solution)/shard_map/reduce_scatter | solution.py:76
  802.9 3.2 copy-start.7
  802.9 3.2 copy-start.8
  802.9 3.2 copy-start.17
  806.1 2.0 copy-start.10
  811.9 0.7 copy-start.38
  811.9 0.8 copy-start.35
  811.9 0.8 copy-start.41
  811.9 1.0 copy-start.31
  811.9 1.0 copy-start.34
  811.9 229.2 %copy-start.45 = (f32[4,1]{0,1:T(1,128)S(1)}, f32[4,1]{0,1:T(1,128)}, u32[]{:S(2)}) copy-start(f32[4,1]{0,1:T(1,128)} %get-tuple-element.175) | copy-start | bytes 52
  811.9 234.3 %copy-start.39 = (bf16[4,2,16]{2,0,1:T(4,128)(2,1)S(1)}, bf16[4,2,16]{2,0,1:T(4,128)(2,1)}, u32[]{:S(2)}) copy-start(bf16[4,2,16]{2,0,1:T(4,128)(2,1)} %copy.67) | copy-start | bytes 772
  811.9 234.5 %copy-start.18 = (f32[4,3072]{1,0:T(4,128)S(1)}, f32[4,3072]{1,0:T(4,128)}, u32[]{:S(2)}) copy-start(f32[4,3072]{1,0:T(4,128)} %reshape.388) | copy-start | bytes 147460
  811.9 234.5 %copy-start.26 = (bf16[1,4,3072]{2,1,0:T(4,128)(2,1)S(1)}, bf16[1,4,3072]{2,1,0:T(4,128)(2,1)}, u32[]{:S(2)}) copy-start(bf16[1,4,3072]{2,1,0:T(4,128)(2,1)} %param.19) | copy-start | bytes 73732
  811.9 234.5 %copy-start.42 = (f32[4]{0:T(128)S(1)}, f32[4]{0:T(128)}, u32[]{:S(2)}) copy-start(f32[4]{0:T(128)} %add_rsqrt_fusion) | copy-start | bytes 52
  812.5 234.9 %copy-start.13 = (bf16[4,48,64]{2,1,0:T(8,128)(2,1)S(1)}, bf16[4,48,64]{2,1,0:T(8,128)(2,1)}, u32[]{:S(2)}) copy-start(bf16[4,48,64]{2,1,0:T(8,128)(2,1)} %copy-done.12) | copy-start | bytes 73732
  1030.9 15.1 %all-to-all-start.3 = ((bf16[8,2,3072]{2,1,0:T(2,128)(2,1)}), bf16[8,2,3072]{2,1,0:T(2,128)(2,1)S(1)}, u32[]{:S(2)}, u32[]{:S(2)}) async-start(bf16[8,2,3072]{2,1,0:T(2,128)(2,1)} %reshape.398), calls=%async_computation.5 | async-start | bytes 196608 | tf_op jit(solution)/shard_map/all_to_all | solution.py:83
  1041.1 189.0 %all-gather.14.cloned.1.call-start = ((), (), s32[]{:S(2)}) async-start(), calls=%async_computation.11 | async-start | bytes 25952256 | tf_op jit(solution)/shard_map/all_gather | solution.py:17
  1041.1 5.9 copy-start.43
  1041.2 9.5 copy-start.11
  1046.1 7.8 copy-start.5
  1046.3 0.6 copy-start.14
  1046.7 0.6 copy-start.19
  1046.7 0.6 copy-start.46
  1047.5 7.6 copy-start.3
  1050.7 5.7 copy-start.23
  1056.4 4.1 copy-start.29
  1058.5 4.0 copy-start.15
  1058.5 4.0 copy-start.20
  1058.5 4.0 copy-start.27
  1058.5 4.0 copy-start.32
  1058.5 4.0 copy-start.44
  1058.5 4.0 copy-start.47
  1230.3 68.9 %copy-start.22 = (f32[128,48]{0,1:T(8,128)S(1)}, f32[128,48]{0,1:T(8,128)}, u32[]{:S(2)}) copy-start(f32[128,48]{0,1:T(8,128)} %copy-done.21) | copy-start | bytes 73732
  1302.7 6.4 copy-start.1
Sparse Core Ops, SparseCore 0:
  14.5 186.7 all-gather.11
  225.3 137.1 all-gather.7
  372.1 217.4 reduce-scatter.2
  731.5 71.4 all-gather.9
  812.1 217.2 reduce-scatter.4
  1050.8 179.2 all-gather.13
